TPU v7x, 512 devices: a whole 4x4x16 slice. The times are simulated.
512 devices in a mesh: state: 16 (over x, y_lo, core), snap: 32 (over y_hi, z).
Axes of the slice: x: 4, y: 4 (y_hi: 2, y_lo: 2; y = y_hi * 2 + y_lo), z: 16, core: 2. Of those that a mesh axis runs over, the one named last changes fastest.
Arguments:
- direct: float32 [8192, 4096], P('state', 'snap'), may hold values from -6 to 6
- adjoint: float32 [8192, 4096], P('state', 'snap'), may hold values from -6 to 6
- cell_weight: float32 [8192], P('state'), may hold values from 0.003314563 to 0.03314563
- right_vecs: float32 [4096, 256], P('snap'), may hold values from -0.09375 to 0.09375
- left_vecs: float32 [4096, 256], P('snap'), may hold values from -0.09375 to 0.09375
- inv_root: float32 [256], replicated, may hold values from 0.5 to 2
Outputs:
- gram: float32 [4096, 4096], P('state', 'snap')
- bal_modes: float32 [8192, 256], P(('state', 'snap'))
- adj_modes: float32 [8192, 256], P(('state', 'snap'))
All inputs are finite; a program needn't handle non-finite values.
Results may differ from a plain program's by a relative error of at most 0.00013.
Values sent between devices are 32-bit elements; how exact they have to be, the bound alone decides.
No kernel may reach another device: no remote copies, remote signals or barrier semaphores. Data moves between devices by JAX's collectives and lax.ppermute only.
A program may use at most 64 MiB of HBM per device.

v0:
```python
import jax
import jax.numpy as jnp
from jax import lax
from jax.sharding import PartitionSpec as P


def local(direct, adjoint, cell_weight, right_vecs, left_vecs, inv_root):
    weighted = adjoint * cell_weight[:, None]
    snap_count = lax.axis_size("snap")
    state_count = lax.axis_size("state")
    local_cols = direct.shape[1]
    total_cols = local_cols * snap_count
    product = lax.dot_general(
        lax.all_gather(weighted, "snap", axis=1, tiled=True),
        direct,
        (((0,), (0,)), ((), ())),
        precision=lax.Precision.HIGHEST,
        preferred_element_type=jnp.float32,
    )
    summed = lax.psum(product, "state")
    row_count = total_cols // state_count
    gram = lax.dynamic_slice_in_dim(summed, lax.axis_index("state") * row_count, row_count, 0)
    bal_terms = jnp.dot(
        direct,
        right_vecs * inv_root[None, :],
        precision=lax.Precision.HIGHEST,
        preferred_element_type=jnp.float32,
    )
    adj_terms = jnp.dot(
        adjoint,
        left_vecs * inv_root[None, :],
        precision=lax.Precision.HIGHEST,
        preferred_element_type=jnp.float32,
    )
    bal_whole, adj_whole = lax.psum((bal_terms, adj_terms), "snap")
    mode_rows = direct.shape[0] // snap_count
    first_row = lax.axis_index("snap") * mode_rows
    bal_modes = lax.dynamic_slice_in_dim(bal_whole, first_row, mode_rows, 0)
    adj_modes = lax.dynamic_slice_in_dim(adj_whole, first_row, mode_rows, 0)
    return (gram, bal_modes, adj_modes)


def solution(mesh):
    in_specs = (
        P("state", "snap"),
        P("state", "snap"),
        P("state"),
        P("snap", None),
        P("snap", None),
        P(),
    )
    out_specs = (P("state", "snap"), P(("state", "snap"), None), P(("state", "snap"), None))
    return jax.shard_map(local, mesh=mesh, in_specs=in_specs, out_specs=out_specs, check_vma=False)
```

profile of v0, /device:TPU:1, one launch (start us, length us, event | category | flops | bytes accessed | tf_op | source)
XLA Modules:
  0.0 670.3 jit_solution(1685941438438533524)
XLA Ops:
  7.2 0.0 copy-start
  7.2 0.0 all-gather.2.cloned.1.call-start
  7.2 1.8 broadcast_multiply_fusion
  9.1 0.0 all-gather.2.cloned.1.call-update
  9.1 0.0 all-reduce.6.cloned.1.call-start
  9.1 2.5 convolution_bitcast_fusion
  11.6 0.0 copy-done
  11.6 2.3 convolution_bitcast_fusion.1
  13.9 0.0 all-reduce.6.cloned.1.call-update
  14.0 0.0 all-reduce.4.cloned.1.call-start
  14.0 201.6 %all-gather.2.cloned.1.call-done = f32[512,4096]{1,0:T(8,128)} async-done(((f32[512,128]{1,0:T(8,128)}), f32[512,4096]{1,0:T(8,128)}) %all-gather.2.cloned.1.call-update) | async-done | bytes 8388624 | tf_op jit(solution)/shard_map/all_gather | solution.py:14
  215.6 16.5 %fusion.4 = f32[4096,128]{1,0:T(8,128)} fusion(f32[512,4096]{1,0:T(8,128)} %all-gather.2.cloned.1.call-done, f32[512,128]{1,0:T(8,128)S(1)} %copy-done), kind=kOutput, calls=%fused_computation.10 | convolution fusion | flops 3221225472 | bytes 10747904 | tf_op jit(solution)/shard_map/dot_general | solution.py:13
  232.1 0.0 all-reduce.4.cloned.1.call-update
  232.2 272.2 %all-reduce.6.cloned.1.call-done = (f32[512,256]{0,1:T(8,128)}, f32[512,256]{0,1:T(8,128)}) async-done(((f32[512,256]{0,1:T(8,128)}, f32[512,256]{0,1:T(8,128)}), (f32[512,256]{0,1:T(8,128)}, f32[512,256]{0,1:T(8,128)})) %all-reduce.6.cloned.1.call-update) | async-done | bytes 1048592 | tf_op jit(solution)/shard_map/psum | solution.py:35
  504.4 1.1 constant_dynamic-slice_fusion
  505.5 0.7 copy.9
  506.2 0.7 copy.10
  506.9 155.3 %all-reduce.4.cloned.1.call-done = f32[4096,128]{1,0:T(8,128)} async-done(((f32[4096,128]{1,0:T(8,128)}), f32[4096,128]{1,0:T(8,128)}) %all-reduce.4.cloned.1.call-update) | async-done | bytes 2097168 | tf_op jit(solution)/shard_map/psum | solution.py:20
  662.2 1.6 constant_dynamic-slice_fusion.2
Async XLA Ops:
  7.2 4.4 copy-start
  7.2 208.4 %all-gather.2.cloned.1.call-start = ((), (), s32[]{:S(2)}) async-start(), calls=%async_computation | async-start | bytes 8650752 | tf_op jit(solution)/shard_map/all_gather | solution.py:14
  9.1 495.3 %all-reduce.6.cloned.1.call-start = ((), (), s32[]{:S(2)}) async-start(), calls=%async_computation.2 | async-start | bytes 2097152 | tf_op jit(solution)/shard_map/psum | solution.py:35
  14.0 648.2 %all-reduce.4.cloned.1.call-start = ((), (), s32[]{:S(2)}) async-start(), calls=%async_computation.1 | async-start | bytes 4194304 | tf_op jit(solution)/shard_map/psum | solution.py:20
Sparse Core Ops, SparseCore 0:
  10.9 204.6 all-gather.1
  218.5 285.8 all-reduce.5
  507.3 154.8 all-reduce.3
where the time goes:
time: 670 us
  waiting for transfers between devices  629 us (94%)
  matrix products  21.3 us (3%)
  between operations  13.8 us (2%)
    psum x1, waiting for transfers between devices, local(): bal_whole, adj_whole = lax.psum((bal_terms, adj_terms), 'snap')  272 us
    all_gather x1, waiting for transfers between devices, local(): lax.all_gather(weighted, 'snap', axis=1, tiled=True)  202 us
    psum x1, waiting for transfers between devices, local(): summed = lax.psum(product, 'state')  155 us
    dot_general x1, matrix products, local(): lax.dot_general(lax.all_gather(weighted, 'snap', axis=1, tiled=True), dir...  16.5 us
  transfers between devices with their start and end apart: 3, of which 3 were waited for; matrix products, arithmetic and copies ran while one was open for 4% of the time, Pallas kernels for 0%

commit v1 on v0

--- a/solution.py
+++ b/solution.py
@@ -17,7 +17,7 @@
         precision=lax.Precision.HIGHEST,
         preferred_element_type=jnp.float32,
     )
-    summed = lax.psum(product, "state")
+    summed = jnp.sum(lax.all_gather(product, "state"), axis=0)
     row_count = total_cols // state_count
     gram = lax.dynamic_slice_in_dim(summed, lax.axis_index("state") * row_count, row_count, 0)
     bal_terms = jnp.dot(

time: 670 us -> 720 us (1.075)
  waiting for transfers between devices: 629 us -> 668 us
  other arithmetic: 1.85 us -> 13.6 us
    all_gather x0 -> x1, waiting for transfers between devices: none -> 194 us  [local(): summed = jnp.sum(lax.all_gather(product, 'state'), axis=0)]
    psum x1 -> x0, waiting for transfers between devices: 155 us -> none  [local(): summed = lax.psum(product, 'state')]
    reduce_sum x0 -> x1, other arithmetic: none -> 11.7 us  [local(): summed = jnp.sum(lax.all_gather(product, 'state'), axis=0)]
  transfers between devices with their start and end apart: 3 -> 3, of which waited for: 3 -> 3; matrix products, arithmetic and copies ran while one was open for 4% -> 3% of each run, Pallas kernels for 0% -> 0%
where the time goes in v1:
time: 720 us
  waiting for transfers between devices  668 us (93%)
  matrix products  21.4 us (3%)
  between operations  13.8 us (2%)
  other arithmetic  13.6 us (2%)
    psum x1, waiting for transfers between devices, local(): bal_whole, adj_whole = lax.psum((bal_terms, adj_terms), 'snap')  272 us
    all_gather x1, waiting for transfers between devices, local(): lax.all_gather(weighted, 'snap', axis=1, tiled=True)  202 us
    all_gather x1, waiting for transfers between devices, local(): summed = jnp.sum(lax.all_gather(product, 'state'), axis=0)  194 us
    dot_general x1, matrix products, local(): lax.dot_general(lax.all_gather(weighted, 'snap', axis=1, tiled=True), dir...  16.6 us
  transfers between devices with their start and end apart: 3, of which 3 were waited for; matrix products, arithmetic and copies ran while one was open for 3% of the time, Pallas kernels for 0%

profile of v1, /device:TPU:1, one launch (start us, length us, event | category | flops | bytes accessed | tf_op | source)
XLA Modules:
  0.0 719.8 jit_solution(18445614418700292004)
XLA Ops:
  7.2 0.0 copy-start
  7.2 0.0 all-gather.4.cloned.1.call-start
  7.2 1.8 broadcast_multiply_fusion
  9.1 0.0 all-gather.4.cloned.1.call-update
  9.1 0.0 all-reduce.3.cloned.1.call-start
  9.1 2.5 convolution_bitcast_fusion
  11.6 0.0 copy-done
  11.6 2.3 convolution_bitcast_fusion.1
  14.0 0.0 all-reduce.3.cloned.1.call-update
  14.0 0.0 all-gather.6.cloned.1.call-start
  14.0 201.6 %all-gather.4.cloned.1.call-done = f32[512,4096]{1,0:T(8,128)} async-done(((f32[512,128]{1,0:T(8,128)}), f32[512,4096]{1,0:T(8,128)}) %all-gather.4.cloned.1.call-update) | async-done | bytes 8388624 | tf_op jit(solution)/shard_map/all_gather | solution.py:14
  215.6 16.6 %fusion.4 = f32[4096,128]{1,0:T(8,128)} fusion(f32[512,4096]{1,0:T(8,128)} %all-gather.4.cloned.1.call-done, f32[512,128]{1,0:T(8,128)S(1)} %copy-done), kind=kOutput, calls=%fused_computation.10 | convolution fusion | flops 3221225472 | bytes 10747904 | tf_op jit(solution)/shard_map/dot_general | solution.py:13
  232.2 0.0 all-gather.6.cloned.1.call-update
  232.2 272.2 %all-reduce.3.cloned.1.call-done = (f32[512,256]{0,1:T(8,128)}, f32[512,256]{0,1:T(8,128)}) async-done(((f32[512,256]{0,1:T(8,128)}, f32[512,256]{0,1:T(8,128)}), (f32[512,256]{0,1:T(8,128)}, f32[512,256]{0,1:T(8,128)})) %all-reduce.3.cloned.1.call-update) | async-done | bytes 1048592 | tf_op jit(solution)/shard_map/psum | solution.py:35
  504.4 1.1 constant_dynamic-slice_fusion
  505.5 0.7 copy.9
  506.2 0.7 copy.10
  506.9 194.0 %all-gather.6.cloned.1.call-done = f32[65536,128]{1,0:T(8,128)} async-done(((f32[4096,128]{1,0:T(8,128)}), f32[65536,128]{1,0:T(8,128)}) %all-gather.6.cloned.1.call-update) | async-done | bytes 33554448 | tf_op jit(solution)/shard_map/all_gather | solution.py:20
  700.8 11.7 %reduce_sum.9 = f32[4096,128]{1,0:T(8,128)S(1)} reduce(f32[16,4096,128]{2,1,0:T(8,128)} %bitcast.9, f32[]{:T(128)} %constant.3.clone.1), dimensions={0}, to_apply=%region_0.0 | reduce | flops 7864320 | bytes 35651588 | tf_op jit(solution)/shard_map/reduce_sum | solution.py:20
  712.6 0.7 constant_dynamic-slice_fusion.2
Async XLA Ops:
  7.2 4.5 copy-start
  7.2 208.4 %all-gather.4.cloned.1.call-start = ((), (), s32[]{:S(2)}) async-start(), calls=%async_computation | async-start | bytes 8650752 | tf_op jit(solution)/shard_map/all_gather | solution.py:14
  9.1 495.3 %all-reduce.3.cloned.1.call-start = ((), (), s32[]{:S(2)}) async-start(), calls=%async_computation.2 | async-start | bytes 2097152 | tf_op jit(solution)/shard_map/psum | solution.py:35
  14.0 686.8 %all-gather.6.cloned.1.call-start = ((), (), s32[]{:S(2)}) async-start(), calls=%async_computation.1 | async-start | bytes 35651584 | tf_op jit(solution)/shard_map/all_gather | solution.py:20
Sparse Core Ops, SparseCore 0:
  10.9 204.6 all-gather.3
  218.5 285.8 all-reduce.2
  506.5 194.2 all-gather.5
